TPU v7x, 32 devices: a whole 2x2x4 slice. The times are simulated.
32 devices in a mesh: tm: 8 (over z, x), space: 4 (over y, core).
Axes of the slice: x: 2, y: 2, z: 4, core: 2. Of those that a mesh axis runs over, the one named last changes fastest.
Arguments:
- guess: float32 [8, 5, 2, 32, 64, 128], P('tm', None, None, 'space'), may hold values from 0 to 1
- feed_rate: float32 [32, 64, 128], P('space'), may hold values from 0.05 to 0.5
- kill_rate: float32 [32, 64, 128], P('space'), may hold values from 0.05 to 0.5
Outputs:
- end_state: float32 [8, 2, 32, 64, 128], P('tm', None, 'space')
- next_nodes: float32 [8, 5, 2, 32, 64, 128], P('tm', None, None, 'space')
All inputs are finite; a program needn't handle non-finite values.
Results may differ from a plain program's by a relative error of at most 0.00002.
Values sent between devices are 32-bit elements; how exact they have to be, the bound alone decides.
A program may use at most 64 MiB of HBM per device.

v0:
```python
import functools
import math

import jax
import jax.numpy as jnp
import numpy as np
from jax import lax
from jax.experimental import pallas as pl
from jax.experimental.pallas import tpu as pltpu
from jax.sharding import PartitionSpec as P

SWEEPS = 4
LAG = 2

substrate_spread = 0.2
catalyst_spread = 0.1
slab_time = 0.5

MESH = pl.DeviceIdType.MESH


def lobatto_table():
    spread_root = math.sqrt(3.0 / 7.0)
    node_times = [0.0, (1.0 - spread_root) / 2.0, 0.5, (1.0 + spread_root) / 2.0, 1.0]
    table = [[0.0] * 5 for blank in range(5)]
    for column in range(5):
        coeffs = [1.0]
        divisor = 1.0
        for other_node in range(5):
            if other_node != column:
                product = [0.0] * (len(coeffs) + 1)
                for power, entry in enumerate(coeffs):
                    product[power + 1] += entry
                    product[power] -= node_times[other_node] * entry
                coeffs = product
                divisor *= node_times[column] - node_times[other_node]
        for row_index in range(5):
            upper = node_times[row_index]
            total_sum = 0.0
            for power, entry in enumerate(coeffs):
                total_sum += entry / (power + 1) * upper ** (power + 1)
            table[row_index][column] = total_sum / divisor
    return (np.array(node_times), np.array(table))


def rates(below, here, above, feed, drain):
    rows, lanes = here[0].shape

    def lap(i):
        w = here[i]
        around = (pltpu.roll(w, 1, 0) + pltpu.roll(w, rows - 1, 0)) + (
            pltpu.roll(w, 1, 1) + pltpu.roll(w, lanes - 1, 1)
        )
        return around + (below[i] + above[i]) - 6.0 * w

    s, c = here
    reacting = s * c * c
    grow_sub = substrate_spread * lap(0) - reacting + feed * (1.0 - s)
    grow_cat = catalyst_spread * lap(1) + reacting - drain * c
    return grow_sub, grow_cat


def kernel(
    slabs, blocks, weights,
    guess, feed_in, kill_in,
    end_out, last_out, rate_out,
    u, last, feed, drain, fbuf,
    load_sem, fixed_sem, tm_send, tm_recv, halo_send, halo_recv, cast_send, cast_recv,
):
    layers = guess.shape[2]
    rows = guess.shape[3]
    tm = lax.axis_index("tm")
    sp = lax.axis_index("space")
    left = lax.rem(sp + blocks - 1, blocks)
    right = lax.rem(sp + 1, blocks)
    top = slabs // 2 - 1
    a = tm // 2
    b = tm % 2
    source = tm == slabs - 1
    not_source = tm < slabs - 1
    primary = 1 - b

    def layer_of(c):
        half = c // 2
        odd = c % 2
        return half + odd * (layers - 1 - 2 * half)

    loads = [
        pltpu.make_async_copy(guess, u.at[0, :, :, pl.ds(1, layers)], load_sem.at[0]),
        pltpu.make_async_copy(feed_in, feed, load_sem.at[1]),
        pltpu.make_async_copy(kill_in, drain, load_sem.at[2]),
    ]
    for load in loads:
        load.start()

    def fixed(k):
        return pltpu.make_async_copy(guess.at[0], u.at[k, 0, :, pl.ds(1, layers)], fixed_sem.at[k - 1])

    @pl.when(tm == 0)
    def _():
        for k in range(1, SWEEPS + 1):
            fixed(k).start()

    barrier = pltpu.get_barrier_semaphore()
    for hop in (1, 2, slabs - 2, slabs - 1):
        pl.semaphore_signal(barrier, inc=1, device_id={"tm": lax.rem(tm + hop, slabs)}, device_id_type=MESH)
    for side in (left, right):
        pl.semaphore_signal(barrier, inc=1, device_id={"space": side}, device_id_type=MESH)
    pl.semaphore_wait(barrier, 6)

    def stream(k, c, src):
        return pltpu.make_async_remote_copy(
            src_ref=src,
            dst_ref=u.at[k + 1, 0, :, 1 + layer_of(c)],
            send_sem=tm_send.at[k, c],
            recv_sem=tm_recv.at[k, c],
            device_id={"tm": lax.rem(tm + 1, slabs)},
            device_id_type=MESH,
        )

    def halo(k, side, src):
        return pltpu.make_async_remote_copy(
            src_ref=src,
            dst_ref=u.at[k, :, :, (1 - side) * (layers + 1)],
            send_sem=halo_send.at[k, side],
            recv_sem=halo_recv.at[k, side],
            device_id={"space": left + side * (right - left)},
            device_id_type=MESH,
        )

    def own_edge(k, side):
        return u.at[k, :, :, 1 + side * (layers - 1)]

    halo(0, 0, guess.at[:, :, 0]).start()
    halo(0, 1, guess.at[:, :, layers - 1]).start()

    @pl.when(not_source)
    def _():
        @pl.loop(0, layers)
        def _(c):
            stream(0, c, guess.at[4, :, layer_of(c)]).start()

    for load in loads:
        load.wait()
    drain[...] = drain[...] + feed[...]

    @pl.when(tm == 0)
    def _():
        for k in range(1, SWEEPS + 1):
            fixed(k).wait()

    def arrive(k, c):
        @pl.when(c == 0)
        def _():
            halo(k, 1, own_edge(k, 1)).wait_recv()

        @pl.when(c == 1)
        def _():
            halo(k, 0, own_edge(k, 0)).wait_recv()

    def begin(k, c):
        @pl.when(tm > 0)
        def _():
            stream(k, c, u.at[k, 4, :, 1 + layer_of(c)]).wait_recv()

    def all_rates(k, i):
        f, d = feed[i], drain[i]
        for j in range(5):
            below, here, above = ((u[k, j, 0, i + n], u[k, j, 1, i + n]) for n in range(3))
            fbuf[j, 0], fbuf[j, 1] = rates(below, here, above, f, d)

    def step(k, i, nodes):
        @pl.loop(0, rows // 8)
        def _(r):
            at = pl.ds(pl.multiple_of(r * 8, 8), 8)
            for s in range(2):
                start = u[k + 1, 0, s, 1 + i, at]
                grown = [fbuf[j, s, at] for j in range(5)]
                for m in nodes:
                    total = grown[0] * weights[m][0]
                    for j in range(1, 5):
                        total = total + grown[j] * weights[m][j]
                    u[k + 1, m, s, 1 + i, at] = start + total

    @pl.loop(0, SWEEPS - 1)
    def _(k):
        @pl.loop(0, layers)
        def _(c):
            i = layer_of(c)
            arrive(k, c)
            all_rates(k, i)
            begin(k, c)
            step(k, i, (4, 1, 2, 3))

            @pl.when(not_source)
            def _():
                stream(k + 1, c, u.at[k + 1, 4, :, 1 + i]).start()

            @pl.when(c < 2)
            def _():
                halo(k + 1, c, own_edge(k + 1, c)).start()

    def cast(lane, c, species, target):
        at = last.at[species, 1 + layer_of(c)]
        return pltpu.make_async_remote_copy(
            src_ref=at,
            dst_ref=at,
            send_sem=cast_send.at[lane, c],
            recv_sem=cast_recv.at[species, c],
            device_id={"tm": target},
            device_id_type=MESH,
        )

    down_on = a > 0
    cross_on = (a < top) | source
    cross_species = primary + jnp.where(source, 1, 0)
    extra_on = tm == 2 * (top - 1)

    def down(c):
        return cast(0, c, primary, lax.rem(tm + slabs - 2, slabs))

    def cross(c):
        return cast(1, c, cross_species, tm + 1 - 2 * b)

    def extra(c):
        return cast(2, c, 0, lax.rem(tm + 2, slabs))

    def last_halo(side):
        return pltpu.make_async_remote_copy(
            src_ref=last.at[:, 1 + side * (layers - 1)],
            dst_ref=last.at[:, (1 - side) * (layers + 1)],
            send_sem=halo_send.at[SWEEPS, side],
            recv_sem=halo_recv.at[SWEEPS, side],
            device_id={"space": left + side * (right - left)},
            device_id_type=MESH,
        )

    @pl.loop(0, layers + LAG)
    def _(c):
        @pl.when(c < layers)
        def _():
            i = layer_of(c)
            arrive(SWEEPS - 1, c)
            all_rates(SWEEPS - 1, i)
            begin(SWEEPS - 1, c)
            step(SWEEPS - 1, i, (4,))
            end_out[:, i] = u[SWEEPS, 4, :, 1 + i]

            @pl.when(source)
            def _():
                last[:, 1 + i] = u[SWEEPS, 4, :, 1 + i]

            @pl.when(not_source)
            def _():
                cast(0, c, primary, tm).wait_recv()

            @pl.when(down_on)
            def _():
                down(c).start()

            @pl.when(cross_on)
            def _():
                cross(c).start()

        @pl.when((c >= LAG) & extra_on)
        def _():
            late = c - LAG
            cast(0, late, 1 - primary, tm).wait_recv()
            extra(late).start()

    def rest(first, stop):
        @pl.when(not_source & (tm != 2 * (top - 1)))
        def _():
            @pl.loop(first, stop)
            def _(c):
                cast(0, c, 1 - primary, tm).wait_recv()

    rest(0, 2)
    last_halo(0).start()
    last_halo(1).start()
    rest(2, layers)
    last_halo(0).wait_recv()
    last_halo(1).wait_recv()

    @pl.loop(0, layers)
    def _(i):
        below, here, above = ((last[0, i + n], last[1, i + n]) for n in range(3))
        grow = rates(below, here, above, feed[i], drain[i])
        for s in range(2):
            last_out[s, i] = here[s]
            rate_out[s, i] = slab_time * grow[s]

    for k in range(SWEEPS):
        for side in range(2):
            halo(k, side, own_edge(k, side)).wait_send()
    last_halo(0).wait_send()
    last_halo(1).wait_send()

    @pl.loop(0, layers)
    def _(c):
        @pl.when(not_source)
        def _():
            for k in range(SWEEPS):
                stream(k, c, u.at[k, 4, :, 1 + layer_of(c)]).wait_send()

        @pl.when(down_on)
        def _():
            down(c).wait_send()

        @pl.when(cross_on)
        def _():
            cross(c).wait_send()

        @pl.when(extra_on)
        def _():
            extra(c).wait_send()


def shards(slabs, blocks, guess, feed_rate, kill_rate):
    node_times, table = lobatto_table()
    weights = [[float(np.float32(slab_time * w)) for w in row] for row in table]
    _, nodes, species, layers, rows, lanes = guess.shape
    pair = jax.ShapeDtypeStruct((species, layers, rows, lanes), jnp.float32)
    dma = pltpu.SemaphoreType.DMA
    end, last, rate = pl.pallas_call(
        functools.partial(kernel, slabs, blocks, weights),
        out_shape=(pair, pair, pair),
        in_specs=[pl.BlockSpec(memory_space=pltpu.HBM)] * 3,
        out_specs=(pl.BlockSpec(memory_space=pltpu.VMEM),) * 3,
        scratch_shapes=[
            pltpu.VMEM((SWEEPS + 1, nodes, species, layers + 2, rows, lanes), jnp.float32),
            pltpu.VMEM((species, layers + 2, rows, lanes), jnp.float32),
            pltpu.VMEM((layers, rows, lanes), jnp.float32),
            pltpu.VMEM((layers, rows, lanes), jnp.float32),
            pltpu.VMEM((nodes, species, rows, lanes), jnp.float32),
            dma((3,)),
            dma((SWEEPS,)),
            dma((SWEEPS, layers)),
            dma((SWEEPS, layers)),
            dma((SWEEPS + 1, 2)),
            dma((SWEEPS + 1, 2)),
            dma((3, layers)),
            dma((2, layers)),
        ],
        compiler_params=pltpu.CompilerParams(
            collective_id=0, has_side_effects=True, vmem_limit_bytes=40 * 1024 * 1024
        ),
    )(guess[0], feed_rate, kill_rate)
    offsets = jnp.asarray(node_times, jnp.float32).reshape((-1, 1, 1, 1, 1))
    next_one = last[None] + offsets * rate[None]
    return (end[None], next_one[None])


def solution(mesh):
    placed = (
        P("tm", None, None, "space", None, None),
        P("space", None, None),
        P("space", None, None),
    )
    return jax.shard_map(
        functools.partial(shards, mesh.shape["tm"], mesh.shape["space"]),
        mesh=mesh,
        in_specs=placed,
        out_specs=(P("tm", None, "space", None, None), P("tm", None, None, "space", None, None)),
        check_vma=False,
    )
```

profile of v0, /device:TPU:0, one launch (start us, length us, event | category | flops | bytes accessed | tf_op | source)
XLA Modules:
  0.0 77.2 jit_solution(16008850762547782299)
XLA Ops:
  0.6 0.0 copy-start.3
  0.6 0.0 copy-start
  0.7 1.7 %copy-done = f32[1,5,2,8,64,128]{5,4,3,2,1,0:T(8,128)S(1)} copy-done((f32[1,5,2,8,64,128]{5,4,3,2,1,0:T(8,128)S(1)}, f32[1,5,2,8,64,128]{5,4,3,2,1,0:T(8,128)}, u32[]{:S(2)}) %copy-start) | copy-done | bytes 2621464
  2.4 0.0 copy-start.1
  2.4 0.9 %copy-done.1 = f32[8,64,128]{2,1,0:T(8,128)S(1)} copy-done((f32[8,64,128]{2,1,0:T(8,128)S(1)}, f32[8,64,128]{2,1,0:T(8,128)}, u32[]{:S(2)}) %copy-start.1) | copy-done | bytes 262168
  3.3 0.0 copy-start.2
  3.3 0.9 %copy-done.2 = f32[8,64,128]{2,1,0:T(8,128)S(1)} copy-done((f32[8,64,128]{2,1,0:T(8,128)S(1)}, f32[8,64,128]{2,1,0:T(8,128)}, u32[]{:S(2)}) %copy-start.2) | copy-done | bytes 262168
  4.3 70.1 %shard_map.59 = (f32[2,8,64,128]{3,2,1,0:T(8,128)S(1)}, f32[2,8,64,128]{3,2,1,0:T(8,128)S(1)}, f32[2,8,64,128]{3,2,1,0:T(8,128)S(1)}) custom-call(f32[5,2,8,64,128]{4,3,2,1,0:T(8,128)S(1)} %bitcast.2, f32[8,64,128]{2,1,0:T(8,128)S(1)} %copy-done.1, f32[8,64,128]{2,1,0:T(8,128)S(1)} %copy-done.2), custom_call_target="tpu_custom_call" | custom-call | tf_op jit(solution)/shard_map/pallas_call | solution.py:325
  74.4 0.0 copy-done.3
  74.5 2.0 %multiply_add_fusion = f32[1,5,2,8,64,128]{5,4,3,2,1,0:T(8,128)} fusion(f32[2,8,64,128]{3,2,1,0:T(8,128)S(1)} %get-tuple-element.7, f32[5]{0:T(128)S(1)} %copy-done.3, f32[2,8,64,128]{3,2,1,0:T(8,128)S(1)} %get-tuple-element.6), kind=kLoop, calls=%fused_computation | loop fusion | flops 1310720 | bytes 3670036 | tf_op jit(solution)/shard_map/add | solution.py:350
  76.4 0.8 %copy.7 = f32[1,2,8,64,128]{4,3,2,1,0:T(8,128)} copy(f32[1,2,8,64,128]{4,3,2,1,0:T(8,128)S(1)} %bitcast.3) | data formatting | bytes 1048576
Async XLA Ops:
  0.6 73.8 %copy-start.3 = (f32[5]{0:T(128)S(1)}, f32[5]{0:T(128)}, u32[]{:S(2)}) copy-start(f32[5]{0:T(128)} %constant.2.clone) | copy-start | bytes 64
  0.6 1.7 %copy-start = (f32[1,5,2,8,64,128]{5,4,3,2,1,0:T(8,128)S(1)}, f32[1,5,2,8,64,128]{5,4,3,2,1,0:T(8,128)}, u32[]{:S(2)}) copy-start(f32[1,5,2,8,64,128]{5,4,3,2,1,0:T(8,128)} %param.4) | copy-start | bytes 7864324
  2.4 0.9 %copy-start.1 = (f32[8,64,128]{2,1,0:T(8,128)S(1)}, f32[8,64,128]{2,1,0:T(8,128)}, u32[]{:S(2)}) copy-start(f32[8,64,128]{2,1,0:T(8,128)} %feed_in.1) | copy-start | bytes 786436
  3.3 0.9 %copy-start.2 = (f32[8,64,128]{2,1,0:T(8,128)S(1)}, f32[8,64,128]{2,1,0:T(8,128)}, u32[]{:S(2)}) copy-start(f32[8,64,128]{2,1,0:T(8,128)} %kill_in.1) | copy-start | bytes 786436
where the time goes:
time: 78.7 us; the launch traced here: 77.2 us
  Pallas kernels  70.1 us (89%)
  local copies, waits for them, and re-layouts  4.44 us (6%)
  other arithmetic  1.95 us (2%)
    pallas_call x1, Pallas kernels, shards(): pl.pallas_call(functools.partial(kernel, slabs, blocks, weights), out_sha...  70.1 us
    unnamed x9, local copies, waits for them, and re-layouts  4.44 us
    add x1, other arithmetic, shards(): next_one = last[None] + offsets * rate[None]  1.95 us

commit v1 on v0

--- a/solution.py
+++ b/solution.py
@@ -314,6 +314,26 @@
         @pl.when(extra_on)
         def _():
             extra(c).wait_send()
+
+
+def finish(offsets, end, last, rate, end_hbm, next_hbm, nodes, sems, end_sem):
+    layers = end.shape[1]
+    end_copy = pltpu.make_async_copy(end, end_hbm, end_sem)
+
+    def out(i):
+        return pltpu.make_async_copy(nodes.at[:, :, i], next_hbm.at[:, :, i], sems.at[i])
+
+    for i in range(layers):
+        for s in range(2):
+            base = last[s, i]
+            grow = rate[s, i]
+            for m in range(5):
+                nodes[m, s, i] = base + offsets[m] * grow
+        out(i).start()
+    end_copy.start()
+    for i in range(layers):
+        out(i).wait()
+    end_copy.wait()
 
 
 def shards(slabs, blocks, guess, feed_rate, kill_rate):
@@ -345,10 +365,22 @@
         compiler_params=pltpu.CompilerParams(
             collective_id=0, has_side_effects=True, vmem_limit_bytes=40 * 1024 * 1024
         ),
-    )(guess[0], feed_rate, kill_rate)
-    offsets = jnp.asarray(node_times, jnp.float32).reshape((-1, 1, 1, 1, 1))
-    next_one = last[None] + offsets * rate[None]
-    return (end[None], next_one[None])
+    )(*(pltpu.with_memory_space_constraint(x, pltpu.HBM) for x in (guess[0], feed_rate, kill_rate)))
+    vmem = pl.BlockSpec(memory_space=pltpu.VMEM)
+    hbm = pl.BlockSpec(memory_space=pltpu.HBM)
+    end_state, next_nodes = pl.pallas_call(
+        functools.partial(finish, [float(np.float32(t)) for t in node_times]),
+        out_shape=(pair, jax.ShapeDtypeStruct((nodes, species, layers, rows, lanes), jnp.float32)),
+        in_specs=[vmem] * 3,
+        out_specs=(hbm, hbm),
+        scratch_shapes=[
+            pltpu.VMEM((nodes, species, layers, rows, lanes), jnp.float32),
+            dma((layers,)),
+            dma(()),
+        ],
+        compiler_params=pltpu.CompilerParams(vmem_limit_bytes=16 * 1024 * 1024),
+    )(end, last, rate)
+    return (end_state[None], next_nodes[None])
 
 
 def solution(mesh):

time: 78.7 us -> 74 us (0.940)
  local copies, waits for them, and re-layouts: 4.44 us -> 0 us
  other arithmetic: 1.95 us -> 0 us
  Pallas kernels: 70.1 us -> 71.9 us
    unnamed x9 -> x0, local copies, waits for them, and re-layouts: 4.44 us -> none
    add x1 -> x0, other arithmetic: 1.95 us -> none  [shards(): next_one = last[None] + offsets * rate[None]]
    pallas_call x0 -> x1, Pallas kernels: none -> 1.75 us  [shards(): pl.pallas_call(functools.partial(finish, [float(np.float32(t)) for t in n...]
where the time goes in v1:
time: 74 us; the launch traced here: 72.6 us
  Pallas kernels  71.9 us (97%)
    pallas_call x1, Pallas kernels, shards(): pl.pallas_call(functools.partial(kernel, slabs, blocks, weights), out_sha...  70.2 us
    pallas_call x1, Pallas kernels, shards(): pl.pallas_call(functools.partial(finish, [float(np.float32(t)) for t in n...  1.75 us

profile of v1, /device:TPU:0, one launch (start us, length us, event | category | flops | bytes accessed | tf_op | source)
XLA Modules:
  0.0 72.6 jit_solution(2016594754511397067)
XLA Ops:
  0.6 70.2 %shard_map.50 = (f32[2,8,64,128]{3,2,1,0:T(8,128)S(1)}, f32[2,8,64,128]{3,2,1,0:T(8,128)S(1)}, f32[2,8,64,128]{3,2,1,0:T(8,128)S(1)}) custom-call(f32[5,2,8,64,128]{4,3,2,1,0:T(8,128)} %bitcast.3, f32[8,64,128]{2,1,0:T(8,128)} %feed_in.1, f32[8,64,128]{2,1,0:T(8,128)} %kill_in.1), custom_call_target="tpu_custom_call" | custom-call | tf_op jit(solution)/shard_map/pallas_call | solution.py:345
  70.8 1.8 %shard_map.51 = (f32[2,8,64,128]{3,2,1,0:T(8,128)}, f32[5,2,8,64,128]{4,3,2,1,0:T(8,128)}) custom-call(f32[2,8,64,128]{3,2,1,0:T(8,128)S(1)} %get-tuple-element.7.end, f32[2,8,64,128]{3,2,1,0:T(8,128)S(1)} %get-tuple-element.8.last, f32[2,8,64,128]{3,2,1,0:T(8,128)S(1)} %get-tuple-element.9.rate), custom_call_target="tpu_custom_call" | custom-call | tf_op jit(solution)/shard_map/pallas_call | solution.py:371

commit v2 on v1

--- a/solution.py
+++ b/solution.py
@@ -10,7 +10,7 @@
 from jax.sharding import PartitionSpec as P
 
 SWEEPS = 4
-LAG = 2
+LEAD = 1
 
 substrate_spread = 0.2
 catalyst_spread = 0.1
@@ -64,49 +64,52 @@
     slabs, blocks, weights,
     guess, feed_in, kill_in,
     end_out, last_out, rate_out,
-    u, last, feed, drain, fbuf,
-    load_sem, fixed_sem, tm_send, tm_recv, halo_send, halo_recv, cast_send, cast_recv,
+    u, last, inc, bay, feed, drain, fbuf,
+    load_sem, fixed_sem, tm_send, tm_recv, halo_send, halo_recv,
+    inc_send, inc_recv, bay_send, bay_recv, cast_send, cast_recv,
 ):
     layers = guess.shape[2]
     rows = guess.shape[3]
+    final = SWEEPS - 1
     tm = lax.axis_index("tm")
     sp = lax.axis_index("space")
     left = lax.rem(sp + blocks - 1, blocks)
     right = lax.rem(sp + 1, blocks)
-    top = slabs // 2 - 1
-    a = tm // 2
-    b = tm % 2
     source = tm == slabs - 1
     not_source = tm < slabs - 1
-    primary = 1 - b
+    second = tm == slabs - 2
+    odd = tm % 2
+    detoured = tm == slabs - 3
 
     def layer_of(c):
         half = c // 2
-        odd = c % 2
-        return half + odd * (layers - 1 - 2 * half)
+        flip = c % 2
+        return half + flip * (layers - 1 - 2 * half)
 
     loads = [
         pltpu.make_async_copy(guess, u.at[0, :, :, pl.ds(1, layers)], load_sem.at[0]),
         pltpu.make_async_copy(feed_in, feed, load_sem.at[1]),
         pltpu.make_async_copy(kill_in, drain, load_sem.at[2]),
     ]
+
+    def fixed(k):
+        return pltpu.make_async_copy(guess.at[0], u.at[k, 0, :, pl.ds(1, layers)], fixed_sem.at[k - 1])
+
+    barrier = pltpu.get_barrier_semaphore()
+    for hop in (1, 2, 3, slabs - 3, slabs - 2, slabs - 1):
+        pl.semaphore_signal(barrier, inc=1, device_id={"tm": lax.rem(tm + hop, slabs)}, device_id_type=MESH)
+    for side in (left, right):
+        pl.semaphore_signal(barrier, inc=1, device_id={"space": side}, device_id_type=MESH)
+
     for load in loads:
         load.start()
-
-    def fixed(k):
-        return pltpu.make_async_copy(guess.at[0], u.at[k, 0, :, pl.ds(1, layers)], fixed_sem.at[k - 1])
 
     @pl.when(tm == 0)
     def _():
         for k in range(1, SWEEPS + 1):
             fixed(k).start()
 
-    barrier = pltpu.get_barrier_semaphore()
-    for hop in (1, 2, slabs - 2, slabs - 1):
-        pl.semaphore_signal(barrier, inc=1, device_id={"tm": lax.rem(tm + hop, slabs)}, device_id_type=MESH)
-    for side in (left, right):
-        pl.semaphore_signal(barrier, inc=1, device_id={"space": side}, device_id_type=MESH)
-    pl.semaphore_wait(barrier, 6)
+    pl.semaphore_wait(barrier, 8)
 
     def stream(k, c, src):
         return pltpu.make_async_remote_copy(
@@ -118,6 +121,26 @@
             device_id_type=MESH,
         )
 
+    def detour(c):
+        return pltpu.make_async_remote_copy(
+            src_ref=u.at[final, 4, :, 1 + layer_of(c)],
+            dst_ref=bay.at[:, layer_of(c)],
+            send_sem=tm_send.at[final, c],
+            recv_sem=bay_recv.at[c],
+            device_id={"tm": 0},
+            device_id_type=MESH,
+        )
+
+    def onward(c):
+        return pltpu.make_async_remote_copy(
+            src_ref=bay.at[:, layer_of(c)],
+            dst_ref=u.at[SWEEPS, 0, :, 1 + layer_of(c)],
+            send_sem=bay_send.at[c],
+            recv_sem=tm_recv.at[final, c],
+            device_id={"tm": slabs - 2},
+            device_id_type=MESH,
+        )
+
     def halo(k, side, src):
         return pltpu.make_async_remote_copy(
             src_ref=src,
@@ -168,6 +191,12 @@
         for j in range(5):
             below, here, above = ((u[k, j, 0, i + n], u[k, j, 1, i + n]) for n in range(3))
             fbuf[j, 0], fbuf[j, 1] = rates(below, here, above, f, d)
+
+    def growth(grown, m):
+        total = grown[0] * weights[m][0]
+        for j in range(1, 5):
+            total = total + grown[j] * weights[m][j]
+        return total
 
     def step(k, i, nodes):
         @pl.loop(0, rows // 8)
@@ -177,12 +206,37 @@
                 start = u[k + 1, 0, s, 1 + i, at]
                 grown = [fbuf[j, s, at] for j in range(5)]
                 for m in nodes:
-                    total = grown[0] * weights[m][0]
-                    for j in range(1, 5):
-                        total = total + grown[j] * weights[m][j]
-                    u[k + 1, m, s, 1 + i, at] = start + total
-
-    @pl.loop(0, SWEEPS - 1)
+                    u[k + 1, m, s, 1 + i, at] = start + growth(grown, m)
+
+    def send_inc(c):
+        at = inc.at[:, layer_of(c)]
+        return pltpu.make_async_remote_copy(
+            src_ref=at,
+            dst_ref=at,
+            send_sem=inc_send.at[c],
+            recv_sem=inc_recv.at[c],
+            device_id={"tm": slabs - 2},
+            device_id_type=MESH,
+        )
+
+    def early(p):
+        inner = jnp.where(p < layers - 4, p + 2, p - (layers - 4))
+        return jnp.where(p < layers - 2, inner, p)
+
+    def foresee(c):
+        i = layer_of(c)
+        arrive(final, c)
+        all_rates(final, i)
+
+        @pl.loop(0, rows // 8)
+        def _(r):
+            at = pl.ds(pl.multiple_of(r * 8, 8), 8)
+            for s in range(2):
+                inc[s, i, at] = growth([fbuf[j, s, at] for j in range(5)], 4)
+
+        send_inc(c).start()
+
+    @pl.loop(0, final)
     def _(k):
         @pl.loop(0, layers)
         def _(c):
@@ -191,39 +245,42 @@
             all_rates(k, i)
             begin(k, c)
             step(k, i, (4, 1, 2, 3))
-
-            @pl.when(not_source)
+            aside = detoured & (k == final - 1)
+
+            @pl.when(not_source & jnp.logical_not(aside))
             def _():
                 stream(k + 1, c, u.at[k + 1, 4, :, 1 + i]).start()
 
+            @pl.when(aside)
+            def _():
+                detour(c).start()
+
             @pl.when(c < 2)
             def _():
                 halo(k + 1, c, own_edge(k + 1, c)).start()
 
-    def cast(lane, c, species, target):
-        at = last.at[species, 1 + layer_of(c)]
+            @pl.when(source & (k == final - 1) & (c >= 4))
+            def _():
+                @pl.loop(c - 4, jnp.where(c == layers - 1, layers, c - 3))
+                def _(p):
+                    foresee(early(p))
+
+    def cast(s, c, target):
+        at = last.at[s, 1 + layer_of(c)]
         return pltpu.make_async_remote_copy(
             src_ref=at,
             dst_ref=at,
-            send_sem=cast_send.at[lane, c],
-            recv_sem=cast_recv.at[species, c],
+            send_sem=cast_send.at[s, c],
+            recv_sem=cast_recv.at[s, c],
             device_id={"tm": target},
             device_id_type=MESH,
         )
 
-    down_on = a > 0
-    cross_on = (a < top) | source
-    cross_species = primary + jnp.where(source, 1, 0)
-    extra_on = tm == 2 * (top - 1)
-
-    def down(c):
-        return cast(0, c, primary, lax.rem(tm + slabs - 2, slabs))
-
-    def cross(c):
-        return cast(1, c, cross_species, tm + 1 - 2 * b)
-
-    def extra(c):
-        return cast(2, c, 0, lax.rem(tm + 2, slabs))
+    def down(s, c):
+        return cast(s, c, lax.rem(tm + slabs - 2, slabs))
+
+    hops = (slabs - 1 - tm) // 2 - jnp.where(odd == 0, LEAD, 0)
+    lag = jnp.where(tm == 0, layers, jnp.minimum(2 * hops, layers))
 
     def last_halo(side):
         return pltpu.make_async_remote_copy(
@@ -235,61 +292,79 @@
             device_id_type=MESH,
         )
 
-    @pl.loop(0, layers + LAG)
-    def _(c):
-        @pl.when(c < layers)
-        def _():
-            i = layer_of(c)
-            arrive(SWEEPS - 1, c)
-            all_rates(SWEEPS - 1, i)
-            begin(SWEEPS - 1, c)
-            step(SWEEPS - 1, i, (4,))
-            end_out[:, i] = u[SWEEPS, 4, :, 1 + i]
-
-            @pl.when(source)
-            def _():
-                last[:, 1 + i] = u[SWEEPS, 4, :, 1 + i]
-
-            @pl.when(not_source)
-            def _():
-                cast(0, c, primary, tm).wait_recv()
-
-            @pl.when(down_on)
-            def _():
-                down(c).start()
-
-            @pl.when(cross_on)
-            def _():
-                cross(c).start()
-
-        @pl.when((c >= LAG) & extra_on)
-        def _():
-            late = c - LAG
-            cast(0, late, 1 - primary, tm).wait_recv()
-            extra(late).start()
-
-    def rest(first, stop):
-        @pl.when(not_source & (tm != 2 * (top - 1)))
-        def _():
-            @pl.loop(first, stop)
-            def _(c):
-                cast(0, c, 1 - primary, tm).wait_recv()
-
-    rest(0, 2)
-    last_halo(0).start()
-    last_halo(1).start()
-    rest(2, layers)
-    last_halo(0).wait_recv()
-    last_halo(1).wait_recv()
-
-    @pl.loop(0, layers)
-    def _(i):
+    def last_rate(c):
+        i = layer_of(c)
         below, here, above = ((last[0, i + n], last[1, i + n]) for n in range(3))
         grow = rates(below, here, above, feed[i], drain[i])
         for s in range(2):
             last_out[s, i] = here[s]
             rate_out[s, i] = slab_time * grow[s]
 
+    def pass_on(p):
+        c = jnp.where(odd == 1, p, early(p))
+        for s in range(2):
+            @pl.when(tm < slabs - 2)
+            def _():
+                cast(s, c, tm).wait_recv()
+
+            @pl.when(tm >= 2)
+            def _():
+                down(s, c).start()
+
+        @pl.when(c == 1)
+        def _():
+            last_halo(0).start()
+            last_halo(1).start()
+
+        @pl.when((p >= layers - 4) & (p < layers - 1))
+        def _():
+            last_rate(p - layers + 6)
+
+    @pl.when(second)
+    def _():
+        @pl.loop(0, layers)
+        def _(p):
+            i = layer_of(early(p))
+            send_inc(early(p)).wait_recv()
+            last[:, 1 + i] = u[final, 4, :, 1 + i] + inc[:, i]
+            pass_on(p)
+
+    @pl.loop(0, 2 * layers)
+    def _(t):
+        @pl.when((tm < slabs - 2) & (t >= lag) & (t < lag + layers))
+        def _():
+            pass_on(t - lag)
+
+        @pl.when((tm == 0) & (t < layers))
+        def _():
+            detour(t).wait_recv()
+            onward(t).start()
+
+        @pl.when(not_source & (t < layers))
+        def _():
+            i = layer_of(t)
+            arrive(final, t)
+            all_rates(final, i)
+            begin(final, t)
+            step(final, i, (4,))
+            end_out[:, i] = u[SWEEPS, 4, :, 1 + i]
+
+        @pl.when(source & (t < layers))
+        def _():
+            i = layer_of(t)
+            begin(final, t)
+            now = u[SWEEPS, 0, :, 1 + i] + inc[:, i]
+            last[:, 1 + i] = now
+            end_out[:, i] = now
+            pass_on(t)
+
+    last_halo(0).wait_recv()
+    last_halo(1).wait_recv()
+
+    @pl.loop(0, layers - 3)
+    def _(j):
+        last_rate(jnp.where(j < 2, j, j + 3))
+
     for k in range(SWEEPS):
         for side in range(2):
             halo(k, side, own_edge(k, side)).wait_send()
@@ -303,17 +378,18 @@
             for k in range(SWEEPS):
                 stream(k, c, u.at[k, 4, :, 1 + layer_of(c)]).wait_send()
 
-        @pl.when(down_on)
-        def _():
-            down(c).wait_send()
-
-        @pl.when(cross_on)
-        def _():
-            cross(c).wait_send()
-
-        @pl.when(extra_on)
-        def _():
-            extra(c).wait_send()
+        @pl.when(source)
+        def _():
+            send_inc(c).wait_send()
+
+        @pl.when(tm == 0)
+        def _():
+            onward(c).wait_send()
+
+        @pl.when(tm >= 2)
+        def _():
+            for s in range(2):
+                down(s, c).wait_send()
 
 
 def finish(offsets, end, last, rate, end_hbm, next_hbm, nodes, sems, end_sem):
@@ -339,17 +415,22 @@
 def shards(slabs, blocks, guess, feed_rate, kill_rate):
     node_times, table = lobatto_table()
     weights = [[float(np.float32(slab_time * w)) for w in row] for row in table]
+    offsets = [float(np.float32(t)) for t in node_times]
     _, nodes, species, layers, rows, lanes = guess.shape
     pair = jax.ShapeDtypeStruct((species, layers, rows, lanes), jnp.float32)
     dma = pltpu.SemaphoreType.DMA
+    vmem = pl.BlockSpec(memory_space=pltpu.VMEM)
+    hbm = pl.BlockSpec(memory_space=pltpu.HBM)
     end, last, rate = pl.pallas_call(
         functools.partial(kernel, slabs, blocks, weights),
-        out_shape=(pair, pair, pair),
-        in_specs=[pl.BlockSpec(memory_space=pltpu.HBM)] * 3,
-        out_specs=(pl.BlockSpec(memory_space=pltpu.VMEM),) * 3,
+        out_shape=(pair,) * 3,
+        in_specs=[hbm] * 3,
+        out_specs=(vmem,) * 3,
         scratch_shapes=[
             pltpu.VMEM((SWEEPS + 1, nodes, species, layers + 2, rows, lanes), jnp.float32),
             pltpu.VMEM((species, layers + 2, rows, lanes), jnp.float32),
+            pltpu.VMEM((species, layers, rows, lanes), jnp.float32),
+            pltpu.VMEM((species, layers, rows, lanes), jnp.float32),
             pltpu.VMEM((layers, rows, lanes), jnp.float32),
             pltpu.VMEM((layers, rows, lanes), jnp.float32),
             pltpu.VMEM((nodes, species, rows, lanes), jnp.float32),
@@ -359,17 +440,19 @@
             dma((SWEEPS, layers)),
             dma((SWEEPS + 1, 2)),
             dma((SWEEPS + 1, 2)),
-            dma((3, layers)),
-            dma((2, layers)),
+            dma((layers,)),
+            dma((layers,)),
+            dma((layers,)),
+            dma((layers,)),
+            dma((species, layers)),
+            dma((species, layers)),
         ],
         compiler_params=pltpu.CompilerParams(
             collective_id=0, has_side_effects=True, vmem_limit_bytes=40 * 1024 * 1024
         ),
     )(*(pltpu.with_memory_space_constraint(x, pltpu.HBM) for x in (guess[0], feed_rate, kill_rate)))
-    vmem = pl.BlockSpec(memory_space=pltpu.VMEM)
-    hbm = pl.BlockSpec(memory_space=pltpu.HBM)
     end_state, next_nodes = pl.pallas_call(
-        functools.partial(finish, [float(np.float32(t)) for t in node_times]),
+        functools.partial(finish, offsets),
         out_shape=(pair, jax.ShapeDtypeStruct((nodes, species, layers, rows, lanes), jnp.float32)),
         in_specs=[vmem] * 3,
         out_specs=(hbm, hbm),

time: 74 us -> 66.6 us (0.90)
  Pallas kernels: 71.9 us -> 65.3 us
    pallas_call x1, Pallas kernels: 70.2 us -> 63.5 us  [shards(): pl.pallas_call(functools.partial(kernel, slabs, blocks, weights), out_sha...]
where the time goes in v2:
time: 66.6 us; the launch traced here: 65.9 us
  Pallas kernels  65.3 us (98%)
    pallas_call x1, Pallas kernels, shards(): pl.pallas_call(functools.partial(kernel, slabs, blocks, weights), out_sha...  63.5 us
    pallas_call x1, Pallas kernels, shards(): pl.pallas_call(functools.partial(finish, offsets), out_shape=(pair, jax.S...  1.75 us

profile of v2, /device:TPU:0, one launch (start us, length us, event | category | flops | bytes accessed | tf_op | source)
XLA Modules:
  0.0 65.9 jit_solution(4938731861900104076)
XLA Ops:
  0.6 63.5 %shard_map.50 = (f32[2,8,64,128]{3,2,1,0:T(8,128)S(1)}, f32[2,8,64,128]{3,2,1,0:T(8,128)S(1)}, f32[2,8,64,128]{3,2,1,0:T(8,128)S(1)}) custom-call(f32[5,2,8,64,128]{4,3,2,1,0:T(8,128)} %bitcast.3, f32[8,64,128]{2,1,0:T(8,128)} %feed_in.1, f32[8,64,128]{2,1,0:T(8,128)} %kill_in.1), custom_call_target="tpu_custom_call" | custom-call | tf_op jit(solution)/shard_map/pallas_call | solution.py:424
  64.2 1.8 %shard_map.51 = (f32[2,8,64,128]{3,2,1,0:T(8,128)}, f32[5,2,8,64,128]{4,3,2,1,0:T(8,128)}) custom-call(f32[2,8,64,128]{3,2,1,0:T(8,128)S(1)} %get-tuple-element.7.end, f32[2,8,64,128]{3,2,1,0:T(8,128)S(1)} %get-tuple-element.8.last, f32[2,8,64,128]{3,2,1,0:T(8,128)S(1)} %get-tuple-element.9.rate), custom_call_target="tpu_custom_call" | custom-call | tf_op jit(solution)/shard_map/pallas_call | solution.py:454

commit v3 on v2

--- a/solution.py
+++ b/solution.py
@@ -10,7 +10,8 @@
 from jax.sharding import PartitionSpec as P
 
 SWEEPS = 4
-LEAD = 1
+FIRST = (2, 1)
+TAILS = (3, 3)
 
 substrate_spread = 0.2
 catalyst_spread = 0.1
@@ -65,8 +66,8 @@
     guess, feed_in, kill_in,
     end_out, last_out, rate_out,
     u, last, inc, bay, feed, drain, fbuf,
-    load_sem, fixed_sem, tm_send, tm_recv, halo_send, halo_recv,
-    inc_send, inc_recv, bay_send, bay_recv, cast_send, cast_recv,
+    load_sem, fixed_sem, tm_send, tm_recv, halo_send, halo_recv, edge_send,
+    inc_send, inc_recv, bay_send, bay_recv, cast_send, back_send, far_send, cast_recv,
 ):
     layers = guess.shape[2]
     rows = guess.shape[3]
@@ -82,9 +83,7 @@
     detoured = tm == slabs - 3
 
     def layer_of(c):
-        half = c // 2
-        flip = c % 2
-        return half + flip * (layers - 1 - 2 * half)
+        return jnp.where(c < 2, c * (layers - 1), c - 1)
 
     loads = [
         pltpu.make_async_copy(guess, u.at[0, :, :, pl.ds(1, layers)], load_sem.at[0]),
@@ -96,7 +95,9 @@
         return pltpu.make_async_copy(guess.at[0], u.at[k, 0, :, pl.ds(1, layers)], fixed_sem.at[k - 1])
 
     barrier = pltpu.get_barrier_semaphore()
-    for hop in (1, 2, 3, slabs - 3, slabs - 2, slabs - 1):
+    jumps = (1, 2, 3, 2 * min(2, slabs // 2 - 1))
+    greeted = sorted({n % slabs for n in jumps} | {-n % slabs for n in jumps})
+    for hop in greeted:
         pl.semaphore_signal(barrier, inc=1, device_id={"tm": lax.rem(tm + hop, slabs)}, device_id_type=MESH)
     for side in (left, right):
         pl.semaphore_signal(barrier, inc=1, device_id={"space": side}, device_id_type=MESH)
@@ -109,34 +110,34 @@
         for k in range(1, SWEEPS + 1):
             fixed(k).start()
 
-    pl.semaphore_wait(barrier, 8)
+    pl.semaphore_wait(barrier, len(greeted) + 2)
 
     def stream(k, c, src):
         return pltpu.make_async_remote_copy(
             src_ref=src,
             dst_ref=u.at[k + 1, 0, :, 1 + layer_of(c)],
-            send_sem=tm_send.at[k, c],
+            send_sem=tm_send.at[k],
             recv_sem=tm_recv.at[k, c],
             device_id={"tm": lax.rem(tm + 1, slabs)},
             device_id_type=MESH,
         )
 
-    def detour(c):
-        return pltpu.make_async_remote_copy(
-            src_ref=u.at[final, 4, :, 1 + layer_of(c)],
-            dst_ref=bay.at[:, layer_of(c)],
-            send_sem=tm_send.at[final, c],
-            recv_sem=bay_recv.at[c],
+    def detour(k, c):
+        return pltpu.make_async_remote_copy(
+            src_ref=u.at[k, 4, :, 1 + layer_of(c)],
+            dst_ref=bay.at[k // 2, :, layer_of(c)],
+            send_sem=tm_send.at[k],
+            recv_sem=bay_recv.at[k // 2, c],
             device_id={"tm": 0},
             device_id_type=MESH,
         )
 
-    def onward(c):
-        return pltpu.make_async_remote_copy(
-            src_ref=bay.at[:, layer_of(c)],
-            dst_ref=u.at[SWEEPS, 0, :, 1 + layer_of(c)],
-            send_sem=bay_send.at[c],
-            recv_sem=tm_recv.at[final, c],
+    def onward(k, c):
+        return pltpu.make_async_remote_copy(
+            src_ref=bay.at[k // 2, :, layer_of(c)],
+            dst_ref=u.at[k + 1, 0, :, 1 + layer_of(c)],
+            send_sem=bay_send.at[k // 2],
+            recv_sem=tm_recv.at[k, c],
             device_id={"tm": slabs - 2},
             device_id_type=MESH,
         )
@@ -145,7 +146,7 @@
         return pltpu.make_async_remote_copy(
             src_ref=src,
             dst_ref=u.at[k, :, :, (1 - side) * (layers + 1)],
-            send_sem=halo_send.at[k, side],
+            send_sem=halo_send,
             recv_sem=halo_recv.at[k, side],
             device_id={"space": left + side * (right - left)},
             device_id_type=MESH,
@@ -213,7 +214,7 @@
         return pltpu.make_async_remote_copy(
             src_ref=at,
             dst_ref=at,
-            send_sem=inc_send.at[c],
+            send_sem=inc_send,
             recv_sem=inc_recv.at[c],
             device_id={"tm": slabs - 2},
             device_id_type=MESH,
@@ -236,61 +237,116 @@
 
         send_inc(c).start()
 
+    depth = slabs // 2 - 1
+    place = (slabs - 1 - tm) // 2
+    entry = jnp.where(odd == 1, min(FIRST[1], depth), min(FIRST[0], depth))
+    rooted = place == 0
+    leads = rooted | ((place >= entry) & (place < depth))
+    backs = (place >= 2) & (place <= entry)
+
+    def cast(s, c, send, hop):
+        at = last.at[s, 1 + layer_of(c)]
+        return pltpu.make_async_remote_copy(
+            src_ref=at,
+            dst_ref=at,
+            send_sem=send,
+            recv_sem=cast_recv.at[s, c],
+            device_id={"tm": lax.rem(tm + slabs + hop, slabs)},
+            device_id_type=MESH,
+        )
+
+    def down(s, c):
+        return cast(s, c, cast_send, jnp.where(rooted, -2 * entry, -2))
+
+    def back(s, c):
+        return cast(s, c, back_send, 2)
+
+    paired = slabs >= 8 and min(FIRST[0], depth) == 2
+    near, deep = TAILS if paired else (0, 0)
+    gives = (tm == 0) | (tm == slabs - 3)
+    spares_down = tm == 3
+    spares_back = tm == slabs - 6
+
+    def across(s, c):
+        return cast(s, c, far_send, jnp.where(tm == 0, 1, -1))
+
+    def last_halo(side):
+        return pltpu.make_async_remote_copy(
+            src_ref=last.at[:, 1 + side * (layers - 1)],
+            dst_ref=last.at[:, (1 - side) * (layers + 1)],
+            send_sem=edge_send,
+            recv_sem=halo_recv.at[SWEEPS, side],
+            device_id={"space": left + side * (right - left)},
+            device_id_type=MESH,
+        )
+
+    def chunk(p):
+        return jnp.where(odd == 1, p, early(p))
+
+    def relay(p):
+        c = chunk(p)
+        for s in range(2):
+            @pl.when(tm < slabs - 2)
+            def _():
+                down(s, c).wait_recv()
+
+            @pl.when(leads & jnp.logical_not(spares_down & (c >= layers - near)))
+            def _():
+                down(s, c).start()
+
+            @pl.when(backs & jnp.logical_not(spares_back & (c >= layers - deep)))
+            def _():
+                back(s, c).start()
+
+            @pl.when(gives & (c >= layers - jnp.where(tm == 0, near, deep)))
+            def _():
+                across(s, c).start()
+
+        @pl.when(c == 1)
+        def _():
+            last_halo(0).start()
+            last_halo(1).start()
+
     @pl.loop(0, final)
     def _(k):
         @pl.loop(0, layers)
         def _(c):
             i = layer_of(c)
+
             arrive(k, c)
             all_rates(k, i)
             begin(k, c)
             step(k, i, (4, 1, 2, 3))
-            aside = detoured & (k == final - 1)
-
-            @pl.when(not_source & jnp.logical_not(aside))
+            away = detoured & ((k == final - 1) | ((k == 0) & (c >= layers // 2)))
+
+
+            @pl.when(not_source & jnp.logical_not(away))
             def _():
                 stream(k + 1, c, u.at[k + 1, 4, :, 1 + i]).start()
 
-            @pl.when(aside)
-            def _():
-                detour(c).start()
+            @pl.when(away)
+            def _():
+                detour(k + 1, c).start()
 
             @pl.when(c < 2)
             def _():
                 halo(k + 1, c, own_edge(k + 1, c)).start()
 
-            @pl.when(source & (k == final - 1) & (c >= 4))
-            def _():
-                @pl.loop(c - 4, jnp.where(c == layers - 1, layers, c - 3))
+            @pl.when((tm == 0) & (k == 0) & (c == layers - 1))
+            def _():
+                @pl.loop(layers // 2, layers)
+                def _(b):
+                    detour(1, b).wait_recv()
+                    onward(1, b).start()
+
+            @pl.when(source & (k == final - 1) & (c >= 3))
+            def _():
+                @pl.loop(c - 3, jnp.where(c == layers - 1, layers - 2, c - 2))
                 def _(p):
                     foresee(early(p))
 
-    def cast(s, c, target):
-        at = last.at[s, 1 + layer_of(c)]
-        return pltpu.make_async_remote_copy(
-            src_ref=at,
-            dst_ref=at,
-            send_sem=cast_send.at[s, c],
-            recv_sem=cast_recv.at[s, c],
-            device_id={"tm": target},
-            device_id_type=MESH,
-        )
-
-    def down(s, c):
-        return cast(s, c, lax.rem(tm + slabs - 2, slabs))
-
-    hops = (slabs - 1 - tm) // 2 - jnp.where(odd == 0, LEAD, 0)
-    lag = jnp.where(tm == 0, layers, jnp.minimum(2 * hops, layers))
-
-    def last_halo(side):
-        return pltpu.make_async_remote_copy(
-            src_ref=last.at[:, 1 + side * (layers - 1)],
-            dst_ref=last.at[:, (1 - side) * (layers + 1)],
-            send_sem=halo_send.at[SWEEPS, side],
-            recv_sem=halo_recv.at[SWEEPS, side],
-            device_id={"space": left + side * (right - left)},
-            device_id_type=MESH,
-        )
+    steps = 1 + jnp.where(place > entry, place - entry, entry - place)
+    lag = jnp.where(tm == 0, layers, jnp.minimum(2 * steps - 2 + 2 * odd, layers))
 
     def last_rate(c):
         i = layer_of(c)
@@ -300,25 +356,19 @@
             last_out[s, i] = here[s]
             rate_out[s, i] = slab_time * grow[s]
 
-    def pass_on(p):
-        c = jnp.where(odd == 1, p, early(p))
-        for s in range(2):
-            @pl.when(tm < slabs - 2)
-            def _():
-                cast(s, c, tm).wait_recv()
-
-            @pl.when(tm >= 2)
-            def _():
-                down(s, c).start()
-
-        @pl.when(c == 1)
-        def _():
-            last_halo(0).start()
-            last_halo(1).start()
-
-        @pl.when((p >= layers - 4) & (p < layers - 1))
-        def _():
-            last_rate(p - layers + 6)
+    def settled(j):
+        plain = jnp.where(j < layers - 2, j + 2, j - layers + 2)
+        return jnp.where(odd == 1, plain, mixed(j))
+
+    def mixed(j):
+        return jnp.where(j < 2, j + 3, jnp.where(j < 3, 2, jnp.where(j < layers - 2, j + 2, j - layers + 2)))
+
+    @pl.when(tm == 0)
+    def _():
+        @pl.loop(0, layers)
+        def _(c):
+            detour(final, c).wait_recv()
+            onward(final, c).start()
 
     @pl.when(second)
     def _():
@@ -327,18 +377,23 @@
             i = layer_of(early(p))
             send_inc(early(p)).wait_recv()
             last[:, 1 + i] = u[final, 4, :, 1 + i] + inc[:, i]
-            pass_on(p)
+            relay(p)
+
+    ready = jnp.where(tm < slabs - 2, layers - 4, 0)
 
     @pl.loop(0, 2 * layers)
     def _(t):
-        @pl.when((tm < slabs - 2) & (t >= lag) & (t < lag + layers))
-        def _():
-            pass_on(t - lag)
-
-        @pl.when((tm == 0) & (t < layers))
-        def _():
-            detour(t).wait_recv()
-            onward(t).start()
+        p = t - lag
+
+        @pl.when((tm < slabs - 2) & (p >= 0) & (p < layers))
+        def _():
+            relay(p)
+
+            gap = jnp.where(odd == 1, 2, layers - 3)
+
+            @pl.when((p >= 2) & (p < layers - 1) & (p != gap))
+            def _():
+                last_rate(settled(p - 2 - jnp.where(p > gap, 1, 0)))
 
         @pl.when(not_source & (t < layers))
         def _():
@@ -352,63 +407,93 @@
         @pl.when(source & (t < layers))
         def _():
             i = layer_of(t)
+
+            @pl.when(t == 2)
+            def _():
+                @pl.loop(layers - 2, layers)
+                def _(c):
+                    foresee(c)
+
             begin(final, t)
             now = u[SWEEPS, 0, :, 1 + i] + inc[:, i]
             last[:, 1 + i] = now
             end_out[:, i] = now
-            pass_on(t)
+            relay(t)
 
     last_halo(0).wait_recv()
     last_halo(1).wait_recv()
 
-    @pl.loop(0, layers - 3)
+    @pl.loop(ready, layers)
     def _(j):
-        last_rate(jnp.where(j < 2, j, j + 3))
-
-    for k in range(SWEEPS):
-        for side in range(2):
-            halo(k, side, own_edge(k, side)).wait_send()
-    last_halo(0).wait_send()
-    last_halo(1).wait_send()
-
-    @pl.loop(0, layers)
-    def _(c):
-        @pl.when(not_source)
-        def _():
-            for k in range(SWEEPS):
-                stream(k, c, u.at[k, 4, :, 1 + layer_of(c)]).wait_send()
-
-        @pl.when(source)
-        def _():
-            send_inc(c).wait_send()
-
+        last_rate(settled(j))
+
+    def drain_sends(ref, sem):
+        pltpu.make_async_copy(ref, ref, sem).wait()
+
+    drain_sends(u.at[pl.ds(0, SWEEPS), :, :, pl.ds(1, 2)], halo_send)
+    drain_sends(last.at[:, pl.ds(1, 2)], edge_send)
+    whole = last.at[:, pl.ds(1, layers)]
+
+    @pl.when(not_source)
+    def _():
+        for k in range(SWEEPS):
+            drain_sends(whole, tm_send.at[k])
+
+    @pl.when(source)
+    def _():
+        drain_sends(whole, inc_send)
+
+    @pl.when(tm == 0)
+    def _():
+        drain_sends(whole, bay_send.at[1])
+        drain_sends(last.at[:, pl.ds(1, layers - layers // 2)], bay_send.at[0])
+
+    @pl.when(leads & jnp.logical_not(spares_down))
+    def _():
+        drain_sends(whole, cast_send)
+
+    @pl.when(leads & spares_down)
+    def _():
+        drain_sends(last.at[:, pl.ds(1, layers - near)], cast_send)
+
+    @pl.when(backs & jnp.logical_not(spares_back))
+    def _():
+        drain_sends(whole, back_send)
+
+    @pl.when(backs & spares_back)
+    def _():
+        drain_sends(last.at[:, pl.ds(1, layers - deep)], back_send)
+
+    if paired:
         @pl.when(tm == 0)
         def _():
-            onward(c).wait_send()
-
-        @pl.when(tm >= 2)
-        def _():
-            for s in range(2):
-                down(s, c).wait_send()
-
-
-def finish(offsets, end, last, rate, end_hbm, next_hbm, nodes, sems, end_sem):
+            drain_sends(last.at[:, pl.ds(1, near)], far_send)
+
+        @pl.when(tm == slabs - 3)
+        def _():
+            drain_sends(last.at[:, pl.ds(1, deep)], far_send)
+
+
+def finish(offsets, end, last, rate, end_hbm, next_hbm, nodes, sems, start_sem, end_sem):
     layers = end.shape[1]
+    start_copy = pltpu.make_async_copy(last, next_hbm.at[0], start_sem)
     end_copy = pltpu.make_async_copy(end, end_hbm, end_sem)
+    start_copy.start()
+    end_copy.start()
 
     def out(i):
-        return pltpu.make_async_copy(nodes.at[:, :, i], next_hbm.at[:, :, i], sems.at[i])
+        return pltpu.make_async_copy(nodes.at[:, :, i], next_hbm.at[pl.ds(1, 4), :, i], sems.at[i])
 
     for i in range(layers):
         for s in range(2):
             base = last[s, i]
             grow = rate[s, i]
-            for m in range(5):
-                nodes[m, s, i] = base + offsets[m] * grow
+            for m in range(1, 5):
+                nodes[m - 1, s, i] = base + offsets[m] * grow
         out(i).start()
-    end_copy.start()
     for i in range(layers):
         out(i).wait()
+    start_copy.wait()
     end_copy.wait()
 
 
@@ -430,21 +515,24 @@
             pltpu.VMEM((SWEEPS + 1, nodes, species, layers + 2, rows, lanes), jnp.float32),
             pltpu.VMEM((species, layers + 2, rows, lanes), jnp.float32),
             pltpu.VMEM((species, layers, rows, lanes), jnp.float32),
-            pltpu.VMEM((species, layers, rows, lanes), jnp.float32),
+            pltpu.VMEM((2, species, layers, rows, lanes), jnp.float32),
             pltpu.VMEM((layers, rows, lanes), jnp.float32),
             pltpu.VMEM((layers, rows, lanes), jnp.float32),
             pltpu.VMEM((nodes, species, rows, lanes), jnp.float32),
             dma((3,)),
             dma((SWEEPS,)),
+            dma((SWEEPS,)),
             dma((SWEEPS, layers)),
-            dma((SWEEPS, layers)),
+            dma(()),
             dma((SWEEPS + 1, 2)),
-            dma((SWEEPS + 1, 2)),
+            dma(()),
+            dma(()),
             dma((layers,)),
-            dma((layers,)),
-            dma((layers,)),
-            dma((layers,)),
-            dma((species, layers)),
+            dma((2,)),
+            dma((2, layers)),
+            dma(()),
+            dma(()),
+            dma(()),
             dma((species, layers)),
         ],
         compiler_params=pltpu.CompilerParams(
@@ -457,8 +545,9 @@
         in_specs=[vmem] * 3,
         out_specs=(hbm, hbm),
         scratch_shapes=[
-            pltpu.VMEM((nodes, species, layers, rows, lanes), jnp.float32),
+            pltpu.VMEM((nodes - 1, species, layers, rows, lanes), jnp.float32),
             dma((layers,)),
+            dma(()),
             dma(()),
         ],
         compiler_params=pltpu.CompilerParams(vmem_limit_bytes=16 * 1024 * 1024),

time: 66.6 us -> 63 us (0.946)
  Pallas kernels: 65.3 us -> 61.1 us
    pallas_call x1, Pallas kernels: 63.5 us -> 59.4 us  [shards(): pl.pallas_call(functools.partial(kernel, slabs, blocks, weights), out_sha...]
where the time goes in v3:
time: 63 us; the launch traced here: 61.8 us
  Pallas kernels  61.1 us (97%)
  between operations  0.64 us (1%)
    pallas_call x1, Pallas kernels, shards(): pl.pallas_call(functools.partial(kernel, slabs, blocks, weights), out_sha...  59.4 us
    pallas_call x1, Pallas kernels, shards(): pl.pallas_call(functools.partial(finish, offsets), out_shape=(pair, jax.S...  1.74 us

profile of v3, /device:TPU:0, one launch (start us, length us, event | category | flops | bytes accessed | tf_op | source)
XLA Modules:
  0.0 61.8 jit_solution(7709238794585741200)
XLA Ops:
  0.6 59.4 %shard_map.50 = (f32[2,8,64,128]{3,2,1,0:T(8,128)S(1)}, f32[2,8,64,128]{3,2,1,0:T(8,128)S(1)}, f32[2,8,64,128]{3,2,1,0:T(8,128)S(1)}) custom-call(f32[5,2,8,64,128]{4,3,2,1,0:T(8,128)} %bitcast.3, f32[8,64,128]{2,1,0:T(8,128)} %feed_in.1, f32[8,64,128]{2,1,0:T(8,128)} %kill_in.1), custom_call_target="tpu_custom_call" | custom-call | tf_op jit(solution)/shard_map/pallas_call | solution.py:509
  60.0 1.7 %shard_map.51 = (f32[2,8,64,128]{3,2,1,0:T(8,128)}, f32[5,2,8,64,128]{4,3,2,1,0:T(8,128)}) custom-call(f32[2,8,64,128]{3,2,1,0:T(8,128)S(1)} %get-tuple-element.7.end, f32[2,8,64,128]{3,2,1,0:T(8,128)S(1)} %get-tuple-element.8.last, f32[2,8,64,128]{3,2,1,0:T(8,128)S(1)} %get-tuple-element.9.rate), custom_call_target="tpu_custom_call" | custom-call | tf_op jit(solution)/shard_map/pallas_call | solution.py:542

commit v4 on v3

--- a/solution.py
+++ b/solution.py
@@ -11,7 +11,8 @@
 
 SWEEPS = 4
 FIRST = (2, 1)
-TAILS = (3, 3)
+NEAR = 4
+DEEP = 2
 
 substrate_spread = 0.2
 catalyst_spread = 0.1
@@ -221,8 +222,8 @@
         )
 
     def early(p):
-        inner = jnp.where(p < layers - 4, p + 2, p - (layers - 4))
-        return jnp.where(p < layers - 2, inner, p)
+        inner = jnp.where(p < layers - 3, p + 2, p - (layers - 3))
+        return jnp.where(p < layers - 1, inner, p)
 
     def foresee(c):
         i = layer_of(c)
@@ -262,10 +263,16 @@
         return cast(s, c, back_send, 2)
 
     paired = slabs >= 8 and min(FIRST[0], depth) == 2
-    near, deep = TAILS if paired else (0, 0)
-    gives = (tm == 0) | (tm == slabs - 3)
+    near = NEAR if paired else 0
+    deep = DEEP if paired else 0
     spares_down = tm == 3
     spares_back = tm == slabs - 6
+
+    def nearby(c):
+        return c >= layers - near
+
+    def offside(c):
+        return (c < deep) | (c >= layers - deep)
 
     def across(s, c):
         return cast(s, c, far_send, jnp.where(tm == 0, 1, -1))
@@ -280,8 +287,10 @@
             device_id_type=MESH,
         )
 
+    plain = jnp.where((tm == slabs - 4) & paired, 1, odd)
+
     def chunk(p):
-        return jnp.where(odd == 1, p, early(p))
+        return jnp.where(plain == 1, p, early(p))
 
     def relay(p):
         c = chunk(p)
@@ -290,21 +299,24 @@
             def _():
                 down(s, c).wait_recv()
 
-            @pl.when(leads & jnp.logical_not(spares_down & (c >= layers - near)))
+            @pl.when(leads & jnp.logical_not(spares_down & nearby(c)))
             def _():
                 down(s, c).start()
 
-            @pl.when(backs & jnp.logical_not(spares_back & (c >= layers - deep)))
+            @pl.when(backs & jnp.logical_not(spares_back & offside(c)))
             def _():
                 back(s, c).start()
 
-            @pl.when(gives & (c >= layers - jnp.where(tm == 0, near, deep)))
+            @pl.when(((tm == 0) & nearby(c)) | ((tm == slabs - 3) & offside(c)))
             def _():
                 across(s, c).start()
 
+        @pl.when(c == 0)
+        def _():
+            last_halo(0).start()
+
         @pl.when(c == 1)
         def _():
-            last_halo(0).start()
             last_halo(1).start()
 
     @pl.loop(0, final)
@@ -341,7 +353,7 @@
 
             @pl.when(source & (k == final - 1) & (c >= 3))
             def _():
-                @pl.loop(c - 3, jnp.where(c == layers - 1, layers - 2, c - 2))
+                @pl.loop(c - 3, jnp.where(c == layers - 1, layers - 1, c - 2))
                 def _(p):
                     foresee(early(p))
 
@@ -357,11 +369,8 @@
             rate_out[s, i] = slab_time * grow[s]
 
     def settled(j):
-        plain = jnp.where(j < layers - 2, j + 2, j - layers + 2)
-        return jnp.where(odd == 1, plain, mixed(j))
-
-    def mixed(j):
-        return jnp.where(j < 2, j + 3, jnp.where(j < 3, 2, jnp.where(j < layers - 2, j + 2, j - layers + 2)))
+        swapped = jnp.where(j < 3, j + 3, jnp.where(j < 4, 2, j + 2))
+        return jnp.where(plain == 1, j + 2, swapped)
 
     @pl.when(tm == 0)
     def _():
@@ -389,11 +398,9 @@
         def _():
             relay(p)
 
-            gap = jnp.where(odd == 1, 2, layers - 3)
-
-            @pl.when((p >= 2) & (p < layers - 1) & (p != gap))
-            def _():
-                last_rate(settled(p - 2 - jnp.where(p > gap, 1, 0)))
+            @pl.when((p >= 2 + plain) & (p < layers - 2 + plain))
+            def _():
+                last_rate(settled(p - 2 - plain))
 
         @pl.when(not_source & (t < layers))
         def _():
@@ -410,9 +417,7 @@
 
             @pl.when(t == 2)
             def _():
-                @pl.loop(layers - 2, layers)
-                def _(c):
-                    foresee(c)
+                foresee(layers - 1)
 
             begin(final, t)
             now = u[SWEEPS, 0, :, 1 + i] + inc[:, i]
@@ -420,12 +425,16 @@
             end_out[:, i] = now
             relay(t)
 
+    @pl.loop(ready, layers - 2)
+    def _(j):
+        last_rate(settled(j))
+
     last_halo(0).wait_recv()
     last_halo(1).wait_recv()
 
-    @pl.loop(ready, layers)
-    def _(j):
-        last_rate(settled(j))
+    @pl.loop(0, 2)
+    def _(c):
+        last_rate(c)
 
     def drain_sends(ref, sem):
         pltpu.make_async_copy(ref, ref, sem).wait()
@@ -462,7 +471,7 @@
 
     @pl.when(backs & spares_back)
     def _():
-        drain_sends(last.at[:, pl.ds(1, layers - deep)], back_send)
+        drain_sends(last.at[:, pl.ds(1, layers - 2 * deep)], back_send)
 
     if paired:
         @pl.when(tm == 0)
@@ -471,7 +480,7 @@
 
         @pl.when(tm == slabs - 3)
         def _():
-            drain_sends(last.at[:, pl.ds(1, deep)], far_send)
+            drain_sends(last.at[:, pl.ds(1, 2 * deep)], far_send)
 
 
 def finish(offsets, end, last, rate, end_hbm, next_hbm, nodes, sems, start_sem, end_sem):

time: 63 us -> 61 us (0.968); the launches traced: 61.8 us -> 60.8 us
  Pallas kernels: 61.1 us -> 60.2 us
    pallas_call x1, Pallas kernels: 59.4 us -> 58.4 us  [shards(): pl.pallas_call(functools.partial(kernel, slabs, blocks, weights), out_sha...]
where the time goes in v4:
time: 61 us; the launch traced here: 60.8 us
  Pallas kernels  60.2 us (99%)
  between operations  0.64 us (1%)
    pallas_call x1, Pallas kernels, shards(): pl.pallas_call(functools.partial(kernel, slabs, blocks, weights), out_sha...  58.4 us
    pallas_call x1, Pallas kernels, shards(): pl.pallas_call(functools.partial(finish, offsets), out_shape=(pair, jax.S...  1.74 us

profile of v4, /device:TPU:0, one launch (start us, length us, event | category | flops | bytes accessed | tf_op | source)
XLA Modules:
  0.0 60.8 jit_solution(7101289217916961639)
XLA Ops:
  0.6 58.4 %shard_map.50 = (f32[2,8,64,128]{3,2,1,0:T(8,128)S(1)}, f32[2,8,64,128]{3,2,1,0:T(8,128)S(1)}, f32[2,8,64,128]{3,2,1,0:T(8,128)S(1)}) custom-call(f32[5,2,8,64,128]{4,3,2,1,0:T(8,128)} %bitcast.3, f32[8,64,128]{2,1,0:T(8,128)} %feed_in.1, f32[8,64,128]{2,1,0:T(8,128)} %kill_in.1), custom_call_target="tpu_custom_call" | custom-call | tf_op jit(solution)/shard_map/pallas_call | solution.py:518
  59.1 1.7 %shard_map.51 = (f32[2,8,64,128]{3,2,1,0:T(8,128)}, f32[5,2,8,64,128]{4,3,2,1,0:T(8,128)}) custom-call(f32[2,8,64,128]{3,2,1,0:T(8,128)S(1)} %get-tuple-element.7.end, f32[2,8,64,128]{3,2,1,0:T(8,128)S(1)} %get-tuple-element.8.last, f32[2,8,64,128]{3,2,1,0:T(8,128)S(1)} %get-tuple-element.9.rate), custom_call_target="tpu_custom_call" | custom-call | tf_op jit(solution)/shard_map/pallas_call | solution.py:551

commit v5 on v4

--- a/solution.py
+++ b/solution.py
@@ -10,6 +10,7 @@
 from jax.sharding import PartitionSpec as P
 
 SWEEPS = 4
+SIDE = 1
 FIRST = (2, 1)
 NEAR = 4
 DEEP = 2
@@ -143,6 +144,26 @@
             device_id_type=MESH,
         )
 
+    def aside(c):
+        return pltpu.make_async_remote_copy(
+            src_ref=guess.at[4, :, layer_of(c)],
+            dst_ref=bay.at[0, :, layer_of(c)],
+            send_sem=tm_send.at[0],
+            recv_sem=bay_recv.at[0, c],
+            device_id={"tm": slabs - 3},
+            device_id_type=MESH,
+        )
+
+    def rejoin(c):
+        return pltpu.make_async_remote_copy(
+            src_ref=bay.at[0, :, layer_of(c)],
+            dst_ref=u.at[1, 0, :, 1 + layer_of(c)],
+            send_sem=bay_send.at[0],
+            recv_sem=tm_recv.at[0, c],
+            device_id={"tm": slabs - 1},
+            device_id_type=MESH,
+        )
+
     def halo(k, side, src):
         return pltpu.make_async_remote_copy(
             src_ref=src,
@@ -159,9 +180,15 @@
     halo(0, 0, guess.at[:, :, 0]).start()
     halo(0, 1, guess.at[:, :, layers - 1]).start()
 
+    @pl.when(second)
+    def _():
+        @pl.loop(layers - SIDE, layers)
+        def _(c):
+            aside(c).start()
+
     @pl.when(not_source)
     def _():
-        @pl.loop(0, layers)
+        @pl.loop(0, jnp.where(second, layers - SIDE, layers))
         def _(c):
             stream(0, c, guess.at[4, :, layer_of(c)]).start()
 
@@ -265,17 +292,17 @@
     paired = slabs >= 8 and min(FIRST[0], depth) == 2
     near = NEAR if paired else 0
     deep = DEEP if paired else 0
-    spares_down = tm == 3
+    spares_down = (tm == 3) | (tm == slabs - 3)
     spares_back = tm == slabs - 6
 
     def nearby(c):
         return c >= layers - near
 
     def offside(c):
-        return (c < deep) | (c >= layers - deep)
+        return (c < deep) | (c >= layers - deep // 2)
 
     def across(s, c):
-        return cast(s, c, far_send, jnp.where(tm == 0, 1, -1))
+        return cast(s, c, far_send, jnp.where(odd == 0, 1, -1))
 
     def last_halo(side):
         return pltpu.make_async_remote_copy(
@@ -307,7 +334,7 @@
             def _():
                 back(s, c).start()
 
-            @pl.when(((tm == 0) & nearby(c)) | ((tm == slabs - 3) & offside(c)))
+            @pl.when((((tm == 0) | (tm == slabs - 6)) & nearby(c)) | ((tm == slabs - 3) & offside(c)))
             def _():
                 across(s, c).start()
 
@@ -318,6 +345,13 @@
         @pl.when(c == 1)
         def _():
             last_halo(1).start()
+
+    @pl.when(detoured)
+    def _():
+        @pl.loop(layers - SIDE, layers)
+        def _(c):
+            aside(c).wait_recv()
+            rejoin(c).start()
 
     @pl.loop(0, final)
     def _(k):
@@ -452,6 +486,10 @@
     def _():
         drain_sends(whole, inc_send)
 
+    @pl.when(detoured)
+    def _():
+        drain_sends(last.at[:, pl.ds(1, SIDE)], bay_send.at[0])
+
     @pl.when(tm == 0)
     def _():
         drain_sends(whole, bay_send.at[1])
@@ -471,16 +509,16 @@
 
     @pl.when(backs & spares_back)
     def _():
-        drain_sends(last.at[:, pl.ds(1, layers - 2 * deep)], back_send)
+        drain_sends(last.at[:, pl.ds(1, layers - deep - deep // 2)], back_send)
 
     if paired:
-        @pl.when(tm == 0)
+        @pl.when((tm == 0) | (tm == slabs - 6))
         def _():
             drain_sends(last.at[:, pl.ds(1, near)], far_send)
 
         @pl.when(tm == slabs - 3)
         def _():
-            drain_sends(last.at[:, pl.ds(1, 2 * deep)], far_send)
+            drain_sends(last.at[:, pl.ds(1, deep + deep // 2)], far_send)
 
 
 def finish(offsets, end, last, rate, end_hbm, next_hbm, nodes, sems, start_sem, end_sem):

time: 61 us -> 60.6 us (level)
  no operation moved by 1% of the time
where the time goes in v5:
time: 60.6 us; the launch traced here: 60.2 us
  Pallas kernels  59.6 us (98%)
  between operations  0.64 us (1%)
    pallas_call x1, Pallas kernels, shards(): pl.pallas_call(functools.partial(kernel, slabs, blocks, weights), out_sha...  57.9 us
    pallas_call x1, Pallas kernels, shards(): pl.pallas_call(functools.partial(finish, offsets), out_shape=(pair, jax.S...  1.74 us

profile of v5, /device:TPU:0, one launch (start us, length us, event | category | flops | bytes accessed | tf_op | source)
XLA Modules:
  0.0 60.2 jit_solution(7068544239570844149)
XLA Ops:
  0.6 57.9 %shard_map.50 = (f32[2,8,64,128]{3,2,1,0:T(8,128)S(1)}, f32[2,8,64,128]{3,2,1,0:T(8,128)S(1)}, f32[2,8,64,128]{3,2,1,0:T(8,128)S(1)}) custom-call(f32[5,2,8,64,128]{4,3,2,1,0:T(8,128)} %bitcast.3, f32[8,64,128]{2,1,0:T(8,128)} %feed_in.1, f32[8,64,128]{2,1,0:T(8,128)} %kill_in.1), custom_call_target="tpu_custom_call" | custom-call | tf_op jit(solution)/shard_map/pallas_call | solution.py:556
  58.5 1.7 %shard_map.51 = (f32[2,8,64,128]{3,2,1,0:T(8,128)}, f32[5,2,8,64,128]{4,3,2,1,0:T(8,128)}) custom-call(f32[2,8,64,128]{3,2,1,0:T(8,128)S(1)} %get-tuple-element.7.end, f32[2,8,64,128]{3,2,1,0:T(8,128)S(1)} %get-tuple-element.8.last, f32[2,8,64,128]{3,2,1,0:T(8,128)S(1)} %get-tuple-element.9.rate), custom_call_target="tpu_custom_call" | custom-call | tf_op jit(solution)/shard_map/pallas_call | solution.py:589

commit v6 on v5

--- a/solution.py
+++ b/solution.py
@@ -299,7 +299,7 @@
         return c >= layers - near
 
     def offside(c):
-        return (c < deep) | (c >= layers - deep // 2)
+        return c < deep
 
     def across(s, c):
         return cast(s, c, far_send, jnp.where(odd == 0, 1, -1))
@@ -509,7 +509,7 @@
 
     @pl.when(backs & spares_back)
     def _():
-        drain_sends(last.at[:, pl.ds(1, layers - deep - deep // 2)], back_send)
+        drain_sends(last.at[:, pl.ds(1, layers - deep)], back_send)
 
     if paired:
         @pl.when((tm == 0) | (tm == slabs - 6))
@@ -518,7 +518,7 @@
 
         @pl.when(tm == slabs - 3)
         def _():
-            drain_sends(last.at[:, pl.ds(1, deep + deep // 2)], far_send)
+            drain_sends(last.at[:, pl.ds(1, deep)], far_send)
 
 
 def finish(offsets, end, last, rate, end_hbm, next_hbm, nodes, sems, start_sem, end_sem):

time: 60.6 us -> 60.4 us (level)
  no operation moved by 1% of the time
where the time goes in v6:
time: 60.4 us; the launch traced here: 60.2 us
  Pallas kernels  59.6 us (99%)
  between operations  0.64 us (1%)
    pallas_call x1, Pallas kernels, shards(): pl.pallas_call(functools.partial(kernel, slabs, blocks, weights), out_sha...  57.9 us
    pallas_call x1, Pallas kernels, shards(): pl.pallas_call(functools.partial(finish, offsets), out_shape=(pair, jax.S...  1.74 us

profile of v6, /device:TPU:0, one launch (start us, length us, event | category | flops | bytes accessed | tf_op | source)
XLA Modules:
  0.0 60.2 jit_solution(12654507920553424468)
XLA Ops:
  0.6 57.9 %shard_map.50 = (f32[2,8,64,128]{3,2,1,0:T(8,128)S(1)}, f32[2,8,64,128]{3,2,1,0:T(8,128)S(1)}, f32[2,8,64,128]{3,2,1,0:T(8,128)S(1)}) custom-call(f32[5,2,8,64,128]{4,3,2,1,0:T(8,128)} %bitcast.3, f32[8,64,128]{2,1,0:T(8,128)} %feed_in.1, f32[8,64,128]{2,1,0:T(8,128)} %kill_in.1), custom_call_target="tpu_custom_call" | custom-call | tf_op jit(solution)/shard_map/pallas_call | solution.py:556
  58.5 1.7 %shard_map.51 = (f32[2,8,64,128]{3,2,1,0:T(8,128)}, f32[5,2,8,64,128]{4,3,2,1,0:T(8,128)}) custom-call(f32[2,8,64,128]{3,2,1,0:T(8,128)S(1)} %get-tuple-element.7.end, f32[2,8,64,128]{3,2,1,0:T(8,128)S(1)} %get-tuple-element.8.last, f32[2,8,64,128]{3,2,1,0:T(8,128)S(1)} %get-tuple-element.9.rate), custom_call_target="tpu_custom_call" | custom-call | tf_op jit(solution)/shard_map/pallas_call | solution.py:589
